TPU v7x, 32 devices: a whole 2x2x4 slice. The times are simulated.
32 devices in a mesh: gx: 4 (over z), gy: 4 (over x, core), gz: 2 (over y).
Axes of the slice: x: 2, y: 2, z: 4, core: 2. Of those that a mesh axis runs over, the one named last changes fastest.
Arguments:
- elevation: float32 [256, 8192], P('gx', ('gy', 'gz')), may hold values from -1 to 1
- surface_potential: float32 [256, 8192], P('gx', ('gy', 'gz')), may hold values from -2 to 2
- seabed: int32 [256, 8192], P('gx', 'gy'), may hold values from 384 to 1023
- interior_potential: float32 [16, 256, 8192], P('gz', 'gx', 'gy'), may hold values from -1.5 to 1.5
Outputs:
- new_elevation: float32 [256, 8192], P('gx', ('gy', 'gz'))
- new_potential: float32 [256, 8192], P('gx', ('gy', 'gz'))
- laplace_apply: float32 [16, 256, 8192], P('gz', 'gx', 'gy')
All inputs are finite; a program needn't handle non-finite values.
Results may differ from a plain program's by a relative error of at most 0.0003.
Values sent between devices are 32-bit elements; how exact they have to be, the bound alone decides.
No kernel may reach another device: no remote copies, remote signals or barrier semaphores. Data moves between devices by JAX's collectives and lax.ppermute only.
A program may use at most 64 MiB of HBM per device.

v0:
```python
import jax
import jax.numpy as jnp
from jax import lax
from jax.sharding import PartitionSpec as P

time_step = 0.05
depth_unit = 0.015625


def with_halo(block, sides, width):
    for axis, dim in sides:
        count = lax.axis_size(axis)
        forward = [(i, i + 1) for i in range(count - 1)]
        forward.append((count - 1, 0))
        backward = [(target, source) for source, target in forward]
        low = lax.ppermute(
            lax.slice_in_dim(block, block.shape[dim] - width, None, axis=dim), axis, forward
        )
        high = lax.ppermute(lax.slice_in_dim(block, 0, width, axis=dim), axis, backward)
        block = jnp.concatenate([low, block, high], axis=dim)
    return block


def partner_2(value, axis, bit):
    mask = 2**bit
    pairs = [(source, source ^ mask) for source in range(lax.axis_size(axis))]
    return lax.ppermute(value, axis, pairs)


def window(extended, step_north, step_east, margin):
    height = extended.shape[-2] - 2 * margin
    breadth = extended.shape[-1] - 2 * margin
    return extended[
        ...,
        margin + step_north : margin + step_north + height,
        margin + step_east : margin + step_east + breadth,
    ]


def rates(extended):
    grad_north = (
        8.0 * (window(extended, 1, 0, 2) - window(extended, -1, 0, 2))
        - (window(extended, 2, 0, 2) - window(extended, -2, 0, 2))
    ) / 12.0
    grad_east = (
        8.0 * (window(extended, 0, 1, 2) - window(extended, 0, -1, 2))
        - (window(extended, 0, 2, 2) - window(extended, 0, -2, 2))
    ) / 12.0
    centre = window(extended, 0, 0, 2)
    poten = extended[1]
    curve_north = (
        -window(poten, 2, 0, 2)
        + 16.0 * window(poten, 1, 0, 2)
        - 30.0 * centre[1]
        + 16.0 * window(poten, -1, 0, 2)
        - window(poten, -2, 0, 2)
    )
    curve_east = (
        -window(poten, 0, 2, 2)
        + 16.0 * window(poten, 0, 1, 2)
        - 30.0 * centre[1]
        + 16.0 * window(poten, 0, -1, 2)
        - window(poten, 0, -2, 2)
    )
    curvature = (curve_north + curve_east) / 12.0
    rate_height = curvature - (grad_north[0] * grad_north[1] + grad_east[0] * grad_east[1])
    rate_potential = -centre[0] - 0.5 * (
        grad_north[1] * grad_north[1] + grad_east[1] * grad_east[1]
    )
    return jnp.stack([rate_height, rate_potential])


def shards(elevation, surface_potential, seabed, interior_potential):
    surface_pair = jnp.stack([elevation, surface_potential])
    depth = seabed.astype(jnp.float32) * depth_unit
    layers = interior_potential.shape[0]
    surface_tile = lax.all_gather(surface_pair, "gz", axis=2, tiled=True)
    triple = jnp.concatenate([surface_tile, depth[None]], 0)
    deep_wide = with_halo(triple, (("gx", 1), ("gy", 2)), 5)
    start_pair = deep_wide[:2]
    section_one = start_pair[:, 2:-2, 2:-2] + time_step * rates(start_pair)
    surface_rim = 0.5 * (
        start_pair[:, 4:-4, 4:-4] + section_one[:, 2:-2, 2:-2] + time_step * rates(section_one)
    )
    depth_rim = deep_wide[2, 4:-4, 4:-4]
    plane_wide = jnp.stack([depth_rim + surface_rim[0], surface_rim[1], depth_rim])
    own_width = surface_pair.shape[2]
    updated = lax.dynamic_slice_in_dim(
        surface_rim[:, 1:-1, 1:-1], lax.axis_index("gz") * own_width, own_width, 2
    )
    volume_wide = with_halo(interior_potential, (("gx", 1), ("gy", 2)), 1)
    layer_group = lax.axis_index("gz")
    bottom_group = layer_group == 0
    outgoing = jnp.where(bottom_group, volume_wide[-1], volume_wide[0])
    partner = partner_2(outgoing, "gz", 0)
    ghost_below = jnp.where(bottom_group, volume_wide[0], partner)
    ghost_above = jnp.where(bottom_group, partner, 2.0 * plane_wide[1] - volume_wide[-1])
    column_stack = jnp.concatenate([ghost_below[None], volume_wide, ghost_above[None]], 0)
    column_centre = plane_wide[0, 1:-1, 1:-1]
    column_north = 0.5 * (plane_wide[0, 2:, 1:-1] - plane_wide[0, :-2, 1:-1])
    column_east = 0.5 * (plane_wide[0, 1:-1, 2:] - plane_wide[0, 1:-1, :-2])
    depth_north = 0.5 * (plane_wide[2, 2:, 1:-1] - plane_wide[2, :-2, 1:-1])
    depth_east = 0.5 * (plane_wide[2, 1:-1, 2:] - plane_wide[2, 1:-1, :-2])
    total_layers = layers * lax.axis_size("gz")
    sigma_level = (
        (layer_group * layers + jnp.arange(layers, dtype=jnp.int32)).astype(jnp.float32) + 0.5
    ) / total_layers
    sigma_level = sigma_level[:, None, None]
    slope_north = (depth_north - sigma_level * column_north) / column_centre
    slope_east = (depth_east - sigma_level * column_east) / column_centre
    spacing = 1.0 / total_layers
    middle_stack = column_stack[1:-1]
    upper_stack = column_stack[2:]
    lower_stack = column_stack[:-2]
    centre = middle_stack[:, 1:-1, 1:-1]
    second_north = middle_stack[:, 2:, 1:-1] - 2.0 * centre + middle_stack[:, :-2, 1:-1]
    second_east = middle_stack[:, 1:-1, 2:] - 2.0 * centre + middle_stack[:, 1:-1, :-2]
    mixed_north = (
        upper_stack[:, 2:, 1:-1]
        - upper_stack[:, :-2, 1:-1]
        - lower_stack[:, 2:, 1:-1]
        + lower_stack[:, :-2, 1:-1]
    ) / (4.0 * spacing)
    mixed_east = (
        upper_stack[:, 1:-1, 2:]
        - upper_stack[:, 1:-1, :-2]
        - lower_stack[:, 1:-1, 2:]
        + lower_stack[:, 1:-1, :-2]
    ) / (4.0 * spacing)
    vertical = (upper_stack[:, 1:-1, 1:-1] - 2.0 * centre + lower_stack[:, 1:-1, 1:-1]) / (
        spacing * spacing
    )
    weight = (
        slope_north * slope_north + slope_east * slope_east + 1.0 / (column_centre * column_centre)
    )
    laplace_apply = (
        second_north
        + second_east
        + 2.0 * slope_north * mixed_north
        + 2.0 * slope_east * mixed_east
        + weight * vertical
    )
    return (updated[0], updated[1], laplace_apply)


def solution(mesh):
    return jax.shard_map(
        shards,
        mesh=mesh,
        in_specs=(P("gx", ("gy", "gz")), P("gx", ("gy", "gz")), P("gx", "gy"), P("gz", "gx", "gy")),
        out_specs=(P("gx", ("gy", "gz")), P("gx", ("gy", "gz")), P("gz", "gx", "gy")),
        check_vma=False,
    )
```

profile of v0, /device:TPU:1, one launch (start us, length us, event | category | flops | bytes accessed | tf_op | source)
XLA Modules:
  0.0 121.5 jit_solution(9207310284389499734)
XLA Ops:
  7.2 0.0 all-gather.2.cloned.1.call-start
  7.2 1.9 %pad_maximum_fusion.24 = f32[2,64,1024]{2,1,0:T(8,128)} fusion(f32[1,64,1024]{2,1,0:T(8,128)} %bitcast.74, f32[1,64,1024]{2,1,0:T(8,128)} %bitcast.75), kind=kLoop, calls=%fused_computation.172 | loop fusion | flops 131072 | bytes 1048576 | tf_op jit(solution)/shard_map/stack | solution.py:74
  9.1 0.0 all-gather.2.cloned.1.call-update
  9.1 1.3 %fusion.87 = (f32[8,1,2048]{2,1,0:T(1,128)S(1)}, f32[8,1,2048]{2,1,0:T(1,128)S(1)}) fusion(f32[8,64,2048]{2,1,0:T(8,128)} %param.7), kind=kLoop, calls=%fused_computation.182 | loop fusion | bytes 262144 | tf_op jit(solution)/shard_map/slice | solution.py:17
  10.4 2.2 %collective-permute-start.5 = (f32[8,1,2048]{2,1,0:T(1,128)S(1)}, f32[8,1,2048]{2,1,0:T(1,128)S(1)}, u32[]{:S(2)}, u32[]{:S(2)}) collective-permute-start(f32[8,1,2048]{2,1,0:T(1,128)S(1)} %get-tuple-element.7), channel_id=1, source_target_pairs={{0,8},{8,16},{16,24},{24,0},{1,9},{9,17},{17,25},{25,1},{2,10},{10... | collective-permute-start | bytes 196616 | tf_op jit(solution)/shard_map/ppermute | solution.py:16
  12.6 2.1 %collective-permute-start.4 = (f32[8,1,2048]{2,1,0:T(1,128)S(1)}, f32[8,1,2048]{2,1,0:T(1,128)S(1)}, u32[]{:S(2)}, u32[]{:S(2)}) collective-permute-start(f32[8,1,2048]{2,1,0:T(1,128)S(1)} %get-tuple-element.8), channel_id=1, source_target_pairs={{8,0},{16,8},{24,16},{0,24},{9,1},{17,9},{25,17},{1,25},{10,2},{18... | collective-permute-start | bytes 196616 | tf_op jit(solution)/shard_map/ppermute | solution.py:19
  14.7 1.1 multiply_bitcast_fusion
  15.8 0.6 collective-permute-done.5
  16.4 0.3 collective-permute-done.4
  16.7 5.5 %pad_maximum_fusion = f32[8,66,2048]{2,1,0:T(8,128)} fusion(f32[8,1,2048]{2,1,0:T(1,128)S(1)} %collective-permute-done.4, f32[8,64,2048]{2,1,0:T(8,128)} %param.7, f32[8,1,2048]{2,1,0:T(1,128)S(1)} %collective-permute-done.5), kind=kLoop, calls=%fused_computation.16 | loop fusion | flops 2162688 | bytes 8650752 | tf_op jit(solution)/shard_map/concatenate | solution.py:20
  22.2 11.1 %all-gather.2.cloned.1.call-done = f32[2,64,2048]{2,1,0:T(8,128)} async-done(((f32[2,64,1024]{2,1,0:T(8,128)}), f32[2,64,2048]{2,1,0:T(8,128)}) %all-gather.2.cloned.1.call-update) | async-done | bytes 1048592 | tf_op jit(solution)/shard_map/all_gather | solution.py:77
  33.3 1.7 %pad_maximum_fusion.26 = (f32[3,5,2048]{2,1,0:T(8,128)}, f32[3,5,2048]{2,1,0:T(8,128)S(1)}) fusion(f32[1,64,2048]{2,1,0:T(8,128)S(1)} %multiply_bitcast_fusion, f32[2,64,2048]{2,1,0:T(8,128)} %all-gather.2.cloned.1.call-done), kind=kLoop, calls=%fused_computation.179 | loop fusion | flops 61440 | bytes 1818624 | tf_op jit(solution)/shard_map/slice | solution.py:17
  35.0 1.2 collective-permute-start
  36.2 2.1 %collective-permute-start.1 = (f32[3,5,2048]{2,1,0:T(8,128)S(1)}, f32[3,5,2048]{2,1,0:T(8,128)S(1)}, u32[]{:S(2)}, u32[]{:S(2)}) collective-permute-start(f32[3,5,2048]{2,1,0:T(8,128)S(1)} %get-tuple-element.16), channel_id=1, source_target_pairs={{8,0},{16,8},{24,16},{0,24},{9,1},{17,9},{25,17},{1,25},{10,2},{18... | collective-permute-start | bytes 368648 | tf_op jit(solution)/shard_map/ppermute | solution.py:19
  38.2 1.2 fusion.86
  39.4 1.5 %collective-permute-start.6 = (f32[8,66,1]{2,1,0:T(8,128)S(1)}, f32[8,66,1]{2,1,0:T(8,128)S(1)}, u32[]{:S(2)}, u32[]{:S(2)}) collective-permute-start(f32[8,66,1]{2,1,0:T(8,128)S(1)} %get-tuple-element.5), channel_id=1, source_target_pairs={{2,0},{4,2},{6,4},{0,6},{3,1},{5,3},{7,5},{1,7},{10,8},{12,10},{14... | collective-permute-start | bytes 6344 | tf_op jit(solution)/shard_map/ppermute | solution.py:19
  40.9 1.1 collective-permute-start.7
  42.0 0.5 add_multiply_fusion
  42.6 7.1 %collective-permute-done.6 = f32[8,66,1]{2,1,0:T(8,128)S(1)} collective-permute-done((f32[8,66,1]{2,1,0:T(8,128)S(1)}, f32[8,66,1]{2,1,0:T(8,128)S(1)}, u32[]{:S(2)}, u32[]{:S(2)}) %collective-permute-start.6) | collective-permute-done | bytes 2144 | tf_op jit(solution)/shard_map/ppermute | solution.py:19
  49.7 7.0 %concatenate.56 = f32[8,66,2050]{2,1,0:T(8,128)} concatenate(f32[8,66,1]{2,1,0:T(8,128)S(1)} %collective-permute-done.7, f32[8,66,2048]{2,1,0:T(8,128)} %pad_maximum_fusion, f32[8,66,1]{2,1,0:T(8,128)S(1)} %collective-permute-done.6), dimensions={2} | concatenate | bytes 8659200 | tf_op jit(solution)/shard_map/concatenate | solution.py:20
  56.6 0.0 collective-permute-done
  56.7 0.3 pad_maximum_fusion.11
  57.0 0.0 copy-start.2
  57.0 0.1 fusion.88
  57.1 0.5 collective-permute-start.3
  57.6 1.3 %collective-permute-start.2 = (f32[3,74,5]{2,1,0:T(8,128)S(1)}, f32[3,74,5]{2,1,0:T(8,128)}, u32[]{:S(2)}, u32[]{:S(2)}) collective-permute-start(f32[3,74,5]{2,1,0:T(8,128)S(1)} %get-tuple-element.14), channel_id=1, source_target_pairs={{0,2},{2,4},{4,6},{6,0},{1,3},{3,5},{5,7},{7,1},{8,10},{10,12},{12... | collective-permute-start | bytes 13328 | tf_op jit(solution)/shard_map/ppermute | solution.py:16
  58.9 2.2 %fusion.75 = f32[66,2050]{1,0:T(8,128)} fusion(f32[8,66,2050]{2,1,0:T(8,128)} %concatenate.56, pred[]{:T(512)S(6)} %eq.3), kind=kLoop, calls=%fused_computation.147 | loop fusion | flops 135300 | bytes 1623601 | tf_op jit(solution)/shard_map/jit(_where)/select_n | solution.py:94
  61.1 0.3 collective-permute-start.8
  61.3 1.8 %collective-permute-done.3 = f32[3,74,5]{2,1,0:T(8,128)S(1)} collective-permute-done((f32[3,74,5]{2,1,0:T(8,128)S(1)}, f32[3,74,5]{2,1,0:T(8,128)S(1)}, u32[]{:S(2)}, u32[]{:S(2)}) %collective-permute-start.3) | collective-permute-done | bytes 4472 | tf_op jit(solution)/shard_map/ppermute | solution.py:19
  63.2 0.6 copy-done.7
  63.8 0.0 collective-permute-done.2
  63.8 3.0 %concatenate.48 = f32[3,74,2058]{2,1,0:T(8,128)S(1)} concatenate(f32[3,74,5]{2,1,0:T(8,128)} %collective-permute-done.2, f32[3,74,2048]{2,1,0:T(8,128)} %copy-done.2, f32[3,74,5]{2,1,0:T(8,128)} %copy-done.7), dimensions={2} | concatenate | bytes 3655008 | tf_op jit(solution)/shard_map/concatenate | solution.py:20
  66.9 2.4 %fusion.41 = (f32[2,70,2054]{2,1,0:T(8,128)S(1)}, f32[2,70,2054]{2,1,0:T(8,128)S(1)}) fusion(f32[3,74,2058]{2,1,0:T(8,128)S(1)} %concatenate.48), kind=kLoop, calls=%fused_computation.78 | loop fusion | flops 2875600 | bytes 11502400 | tf_op jit(solution)/shard_map/div | solution.py:41
  69.3 0.3 fusion.61
  69.6 1.4 %fusion.65 = f32[1,70,2054]{2,1,0:T(8,128)S(1)} fusion(f32[2,70,2054]{2,1,0:T(8,128)S(1)} %get-tuple-element.10, f32[2,70,2054]{2,1,0:T(8,128)S(1)} %get-tuple-element.9, f32[74,2058]{1,0:T(8,128)S(1)} %slice_bitcast_fusion, f32[3,74,2058]{2,1,0:T(8,128)S(1)} %concatenate.48), kind=kLoop, calls=%fused_computation.126 | loop fusion | flops 3019380 | bytes 8051680 | tf_op jit(solution)/shard_map/stack | solution.py:70
  71.0 0.4 slice_add_fusion.1
  71.4 2.4 %fusion.33 = (f32[2,66,2050]{2,1,0:T(8,128)S(1)}, f32[2,66,2050]{2,1,0:T(8,128)S(1)}) fusion(f32[2,70,2054]{2,1,0:T(8,128)S(1)} %slice_add_fusion.1), kind=kLoop, calls=%fused_computation.65 | loop fusion | flops 2706000 | bytes 10824000 | tf_op jit(solution)/shard_map/div | solution.py:41
  73.9 0.3 fusion.47
  74.2 1.4 %fusion.51 = f32[1,66,2050]{2,1,0:T(8,128)S(1)} fusion(f32[2,66,2050]{2,1,0:T(8,128)S(1)} %get-tuple-element.18, f32[2,66,2050]{2,1,0:T(8,128)S(1)} %get-tuple-element.17, f32[70,2054]{1,0:T(8,128)S(1)} %slice_bitcast_fusion.3, f32[2,70,2054]{2,1,0:T(8,128)S(1)} %slice_add_fusion.1), kind=kLoop, calls=%fused_computation.99 | loop fusion | flops 2841300 | bytes 7576800 | tf_op jit(solution)/shard_map/stack | solution.py:70
  75.6 0.0 copy-start.8
  75.6 0.7 fusion.36
  76.3 0.2 slice_add_fusion.2
  76.6 0.3 slice.461
  77.0 2.5 %fusion.85 = (f32[64,2048]{1,0:T(8,128)}, f32[64,2048]{1,0:T(8,128)}) fusion(f32[3,5,2048]{2,1,0:T(8,128)S(1)} %collective-permute-done, f32[1,64,2048]{2,1,0:T(8,128)S(1)} %copy-done.4, f32[2,64,2048]{2,1,0:T(8,128)S(1)} %copy-done.1, f32[3,5,2048]{2,1,0:T(8,128)S(1)} %collective-permute-done.1, f32[3,74,5]{2,1,0:T(8,128)} %collective-permute-done.2, ...), kind=kLoop, calls=%fused_computation.168 | loop fusion | flops 2097152 | bytes 2876080 | tf_op jit(solution)/shard_map/sub | solution.py:109
  79.4 0.8 dynamic-slice_bitcast_fusion
  80.2 2.0 %fusion.82 = (f32[64,2048]{1,0:T(8,128)}, f32[64,2048]{1,0:T(8,128)}, f32[64,2048]{1,0:T(8,128)}, f32[64,2048]{1,0:T(8,128)}) fusion(f32[1,66,2050]{2,1,0:T(8,128)S(1)} %slice_add_fusion.2), kind=kLoop, calls=%fused_computation.164 | loop fusion | flops 786432 | bytes 4718592 | tf_op jit(solution)/shard_map/mul | solution.py:109
  82.2 2.1 %fusion.46 = (f32[1,66,2050]{2,1,0:T(8,128)S(1)}, f32[1,66,2050]{2,1,0:T(8,128)}) fusion(f32[66,2050]{1,0:T(8,128)} %collective-permute-done.8, f32[2,66,2050]{2,1,0:T(8,128)S(1)} %fusion.36, f32[8,66,2050]{2,1,0:T(8,128)S(1)} %bitcast.73, pred[]{:T(512)S(6)} %eq.3), kind=kLoop, calls=%fused_computation.89 | loop fusion | flops 541200 | bytes 3247201 | tf_op jit(solution)/shard_map/broadcast_in_dim | solution.py:98
  84.3 30.3 %fusion.5 = f32[8,64,2048]{2,1,0:T(8,128)} fusion(f32[8,66,2050]{2,1,0:T(8,128)S(1)} %bitcast.73, f32[1,66,2050]{2,1,0:T(8,128)} %get-tuple-element.4, f32[1,66,2050]{2,1,0:T(8,128)S(1)} %get-tuple-element.3, f32[8,66,1]{2,1,0:T(8,128)} %copy-done.6, f32[8,1,2048]{2,1,0:T(1,128)} %copy-done.11, f32[8,64,2048]{2,1,0:T(8,128)S(1)} %copy-done, ...), kind=kLoop, calls=%fused_computation.22 | loop fusion | flops 55574528 | bytes 17081664 | tf_op jit(solution)/shard_map/add | solution.py:137
  (31 shorter events, 0.1 us)
Async XLA Ops:
  7.2 26.1 %all-gather.2.cloned.1.call-start = ((), (), s32[]{:S(2)}) async-start(), calls=%async_computation | async-start | bytes 1572864 | tf_op jit(solution)/shard_map/all_gather | solution.py:77
  10.4 5.9 %collective-permute-start.5 = (f32[8,1,2048]{2,1,0:T(1,128)S(1)}, f32[8,1,2048]{2,1,0:T(1,128)S(1)}, u32[]{:S(2)}, u32[]{:S(2)}) collective-permute-start(f32[8,1,2048]{2,1,0:T(1,128)S(1)} %get-tuple-element.7), channel_id=1, source_target_pairs={{0,8},{8,16},{16,24},{24,0},{1,9},{9,17},{17,25},{25,1},{2,10},{10... | collective-permute-start | bytes 196616 | tf_op jit(solution)/shard_map/ppermute | solution.py:16
  12.6 4.1 %collective-permute-start.4 = (f32[8,1,2048]{2,1,0:T(1,128)S(1)}, f32[8,1,2048]{2,1,0:T(1,128)S(1)}, u32[]{:S(2)}, u32[]{:S(2)}) collective-permute-start(f32[8,1,2048]{2,1,0:T(1,128)S(1)} %get-tuple-element.8), channel_id=1, source_target_pairs={{8,0},{16,8},{24,16},{0,24},{9,1},{17,9},{25,17},{1,25},{10,2},{18... | collective-permute-start | bytes 196616 | tf_op jit(solution)/shard_map/ppermute | solution.py:19
  15.8 40.9 %copy-start.3 = (f32[1,64,2048]{2,1,0:T(8,128)}, f32[1,64,2048]{2,1,0:T(8,128)S(1)}, u32[]{:S(2)}) copy-start(f32[1,64,2048]{2,1,0:T(8,128)S(1)} %multiply_bitcast_fusion) | copy-start | bytes 1572868
  16.4 5.8 %copy-start.9 = (f32[8,1,2048]{2,1,0:T(1,128)}, f32[8,1,2048]{2,1,0:T(1,128)S(1)}, u32[]{:S(2)}) copy-start(f32[8,1,2048]{2,1,0:T(1,128)S(1)} %collective-permute-done.5) | copy-start | bytes 196612
  16.7 5.5 %copy-start.11 = (f32[8,1,2048]{2,1,0:T(1,128)}, f32[8,1,2048]{2,1,0:T(1,128)S(1)}, u32[]{:S(2)}) copy-start(f32[8,1,2048]{2,1,0:T(1,128)S(1)} %collective-permute-done.4) | copy-start | bytes 196612
  35.0 21.7 %collective-permute-start = (f32[3,5,2048]{2,1,0:T(8,128)}, f32[3,5,2048]{2,1,0:T(8,128)S(1)}, u32[]{:S(2)}, u32[]{:S(2)}) collective-permute-start(f32[3,5,2048]{2,1,0:T(8,128)} %get-tuple-element.15), channel_id=1, source_target_pairs={{0,8},{8,16},{16,24},{24,0},{1,9},{9,17},{17,25},{25,1},{2,10},{10... | collective-permute-start | bytes 368648 | tf_op jit(solution)/shard_map/ppermute | solution.py:16
  36.2 20.5 %collective-permute-start.1 = (f32[3,5,2048]{2,1,0:T(8,128)S(1)}, f32[3,5,2048]{2,1,0:T(8,128)S(1)}, u32[]{:S(2)}, u32[]{:S(2)}) collective-permute-start(f32[3,5,2048]{2,1,0:T(8,128)S(1)} %get-tuple-element.16), channel_id=1, source_target_pairs={{8,0},{16,8},{24,16},{0,24},{9,1},{17,9},{25,17},{1,25},{10,2},{18... | collective-permute-start | bytes 368648 | tf_op jit(solution)/shard_map/ppermute | solution.py:19
  39.4 10.2 %collective-permute-start.6 = (f32[8,66,1]{2,1,0:T(8,128)S(1)}, f32[8,66,1]{2,1,0:T(8,128)S(1)}, u32[]{:S(2)}, u32[]{:S(2)}) collective-permute-start(f32[8,66,1]{2,1,0:T(8,128)S(1)} %get-tuple-element.5), channel_id=1, source_target_pairs={{2,0},{4,2},{6,4},{0,6},{3,1},{5,3},{7,5},{1,7},{10,8},{12,10},{14... | collective-permute-start | bytes 6344 | tf_op jit(solution)/shard_map/ppermute | solution.py:19
  40.9 8.8 %collective-permute-start.7 = (f32[8,66,1]{2,1,0:T(8,128)S(1)}, f32[8,66,1]{2,1,0:T(8,128)S(1)}, u32[]{:S(2)}, u32[]{:S(2)}) collective-permute-start(f32[8,66,1]{2,1,0:T(8,128)S(1)} %get-tuple-element.6), channel_id=1, source_target_pairs={{0,2},{2,4},{4,6},{6,0},{1,3},{3,5},{5,7},{7,1},{8,10},{10,12},{12... | collective-permute-start | bytes 6344 | tf_op jit(solution)/shard_map/ppermute | solution.py:16
  42.6 14.1 %copy-start.1 = (f32[2,64,2048]{2,1,0:T(8,128)S(1)}, f32[2,64,2048]{2,1,0:T(8,128)}, u32[]{:S(2)}) copy-start(f32[2,64,2048]{2,1,0:T(8,128)} %all-gather.2.cloned.1.call-done) | copy-start | bytes 3145732
  49.7 7.0 %copy-start.5 = (f32[8,66,1]{2,1,0:T(8,128)}, f32[8,66,1]{2,1,0:T(8,128)S(1)}, u32[]{:S(2)}) copy-start(f32[8,66,1]{2,1,0:T(8,128)S(1)} %collective-permute-done.6) | copy-start | bytes 6340
  49.7 7.0 %copy-start.6 = (f32[8,66,1]{2,1,0:T(8,128)}, f32[8,66,1]{2,1,0:T(8,128)S(1)}, u32[]{:S(2)}) copy-start(f32[8,66,1]{2,1,0:T(8,128)S(1)} %collective-permute-done.7) | copy-start | bytes 6340
  57.0 6.2 %copy-start.2 = (f32[3,74,2048]{2,1,0:T(8,128)}, f32[3,74,2048]{2,1,0:T(8,128)S(1)}, u32[]{:S(2)}) copy-start(f32[3,74,2048]{2,1,0:T(8,128)S(1)} %pad_maximum_fusion.11) | copy-start | bytes 5455876
  57.1 6.1 %collective-permute-start.3 = (f32[3,74,5]{2,1,0:T(8,128)S(1)}, f32[3,74,5]{2,1,0:T(8,128)S(1)}, u32[]{:S(2)}, u32[]{:S(2)}) collective-permute-start(f32[3,74,5]{2,1,0:T(8,128)S(1)} %get-tuple-element.13), channel_id=1, source_target_pairs={{2,0},{4,2},{6,4},{0,6},{3,1},{5,3},{7,5},{1,7},{10,8},{12,10},{14... | collective-permute-start | bytes 13328 | tf_op jit(solution)/shard_map/ppermute | solution.py:19
  57.6 6.2 %collective-permute-start.2 = (f32[3,74,5]{2,1,0:T(8,128)S(1)}, f32[3,74,5]{2,1,0:T(8,128)}, u32[]{:S(2)}, u32[]{:S(2)}) collective-permute-start(f32[3,74,5]{2,1,0:T(8,128)S(1)} %get-tuple-element.14), channel_id=1, source_target_pairs={{0,2},{2,4},{4,6},{6,0},{1,3},{3,5},{5,7},{7,1},{8,10},{10,12},{12... | collective-permute-start | bytes 13328 | tf_op jit(solution)/shard_map/ppermute | solution.py:16
  61.1 21.1 %collective-permute-start.8 = (f32[66,2050]{1,0:T(8,128)}, f32[66,2050]{1,0:T(8,128)}, u32[]{:S(2)}, u32[]{:S(2)}) collective-permute-start(f32[66,2050]{1,0:T(8,128)} %fusion.75), channel_id=1, source_target_pairs={{0,1},{1,0},{2,3},{3,2},{4,5},{5,4},{6,7},{7,6},{8,9},{9,8},{10,11... | collective-permute-start | bytes 1623608 | tf_op jit(solution)/shard_map/ppermute | solution.py:27
  63.2 0.6 copy-start.7
  75.6 1.4 %copy-start.4 = (f32[1,64,2048]{2,1,0:T(8,128)S(1)}, f32[1,64,2048]{2,1,0:T(8,128)}, u32[]{:S(2)}) copy-start(f32[1,64,2048]{2,1,0:T(8,128)} %copy-done.3) | copy-start | bytes 1572868
  75.6 1.4 %copy-start.8 = (f32[3,74,5]{2,1,0:T(8,128)S(1)}, f32[3,74,5]{2,1,0:T(8,128)}, u32[]{:S(2)}) copy-start(f32[3,74,5]{2,1,0:T(8,128)} %copy-done.7) | copy-start | bytes 13324
  76.3 5.9 %slice-start = ((s8[5013504]{0:T(1024)(128)(4,1)}), s8[4194304]{0:T(1024)(128)(4,1)S(1)}, s32[]{:S(2)}) async-start(s8[5013504]{0:T(1024)(128)(4,1)} %bitcast.72), calls=%async_computation.1 | async-start | bytes 8388608
  76.9 5.3 %slice-start.1 = ((s8[5013504]{0:T(1024)(128)(4,1)}), s8[819200]{0:T(1024)(128)(4,1)S(1)}, s32[]{:S(2)}) async-start(s8[5013504]{0:T(1024)(128)(4,1)} %bitcast.72), calls=%async_computation.2 | async-start | bytes 1638400
  80.2 4.1 %copy-start = (f32[8,64,2048]{2,1,0:T(8,128)S(1)}, f32[8,64,2048]{2,1,0:T(8,128)}, u32[]{:S(2)}) copy-start(f32[8,64,2048]{2,1,0:T(8,128)} %param.7) | copy-start | bytes 12582916
  80.2 4.1 %copy-start.10 = (f32[8,1,2048]{2,1,0:T(1,128)S(1)}, f32[8,1,2048]{2,1,0:T(1,128)}, u32[]{:S(2)}) copy-start(f32[8,1,2048]{2,1,0:T(1,128)} %copy-done.9) | copy-start | bytes 196612
Sparse Core Ops, SparseCore 0:
  10.1 23.1 all-gather.1
where the time goes:
time: 122 us; the launch traced here: 121 us
  other arithmetic  59.5 us (49%)
  waiting for transfers between devices  21 us (17%)
  local copies, waits for them, and re-layouts  14.5 us (12%)
  between operations  14.3 us (12%)
  starting transfers between devices  12.2 us (10%)
    add x1, other arithmetic, shards(): second_north + second_east + 2.0 * slope_north * mixed_north  30.3 us
    all_gather x1, waiting for transfers between devices, shards(): surface_tile = lax.all_gather(surface_pair, 'gz', axis=2, tiled=True)  11.1 us
    concatenate x2, local copies, waits for them, and re-layouts, with_halo(): block = jnp.concatenate([low, block, high], axis=dim)  9.94 us
    ppermute x4, waiting for transfers between devices, with_halo(): lax.ppermute(lax.slice_in_dim(block, 0, width, axis=dim), axis, backward)  9.24 us
    ppermute x4, starting transfers between devices, with_halo(): lax.ppermute(lax.slice_in_dim(block, 0, width, axis=dim), axis, backward)  6.1 us
    concatenate x2, other arithmetic, with_halo(): block = jnp.concatenate([low, block, high], axis=dim)  5.81 us
    ppermute x4, starting transfers between devices, with_halo(): lax.ppermute(lax.slice_in_dim(block, block.shape[dim] - width, None, axis...  5.81 us
    div x2, other arithmetic, rates(): (8.0 * (window(extended, 1, 0, 2) - window(extended, -1, 0, 2)) - (window...  4.83 us
  transfers between devices with their start and end apart: 10, of which 5 were waited for; matrix products, arithmetic and copies ran while one was open for 30% of the time, Pallas kernels for 0%

commit v1 on v0

--- a/solution.py
+++ b/solution.py
@@ -74,7 +74,14 @@
     surface_pair = jnp.stack([elevation, surface_potential])
     depth = seabed.astype(jnp.float32) * depth_unit
     layers = interior_potential.shape[0]
-    surface_tile = lax.all_gather(surface_pair, "gz", axis=2, tiled=True)
+    ways, here = (lax.axis_size("gz"), lax.axis_index("gz"))
+    surface_tile, reach = (surface_pair, 1)
+    while reach < ways:
+        theirs = lax.ppermute(surface_tile, "gz", [(d, d ^ reach) for d in range(ways)])
+        mine_first = jnp.concatenate([surface_tile, theirs], axis=2)
+        theirs_first = jnp.concatenate([theirs, surface_tile], axis=2)
+        surface_tile = jnp.where(here & reach == 0, mine_first, theirs_first)
+        reach = 2 * reach
     triple = jnp.concatenate([surface_tile, depth[None]], 0)
     deep_wide = with_halo(triple, (("gx", 1), ("gy", 2)), 5)
     start_pair = deep_wide[:2]

time: 122 us -> 101 us (0.83)
  between operations: 14.3 us -> 1.1 us
  waiting for transfers between devices: 21 us -> 14.8 us
  other arithmetic: 59.5 us -> 55.4 us
  starting transfers between devices: 12.2 us -> 15.4 us
    all_gather x1 -> x0, waiting for transfers between devices: 11.1 us -> none  [shards(): surface_tile = lax.all_gather(surface_pair, 'gz', axis=2, tiled=True)]
    ppermute x0 -> x1, waiting for transfers between devices: none -> 6.98 us  [shards(): lax.ppermute(surface_tile, 'gz', [(d, d ^ reach) for d in range(ways)])]
    concatenate x2, other arithmetic: 5.81 us -> 3.41 us  [with_halo(): block = jnp.concatenate([low, block, high], axis=dim)]
    ppermute x4, starting transfers between devices: 6.1 us -> 8.13 us  [with_halo(): lax.ppermute(lax.slice_in_dim(block, 0, width, axis=dim), axis, backward)]
    ppermute x4, waiting for transfers between devices: 9.24 us -> 7.84 us  [with_halo(): lax.ppermute(lax.slice_in_dim(block, 0, width, axis=dim), axis, backward)]
    ppermute x0 -> x1, starting transfers between devices: none -> 1.3 us  [shards(): lax.ppermute(surface_tile, 'gz', [(d, d ^ reach) for d in range(ways)])]
  transfers between devices with their start and end apart: 10 -> 10, of which waited for: 5 -> 3; matrix products, arithmetic and copies ran while one was open for 30% -> 33% of each run, Pallas kernels for 0% -> 0%
where the time goes in v1:
time: 101 us; the launch traced here: 100 us
  other arithmetic  55.4 us (55%)
  starting transfers between devices  15.4 us (15%)
  waiting for transfers between devices  14.8 us (15%)
  local copies, waits for them, and re-layouts  13.5 us (13%)
  between operations  1.1 us (1%)
    add x1, other arithmetic, shards(): second_north + second_east + 2.0 * slope_north * mixed_north  30.2 us
    concatenate x2, local copies, waits for them, and re-layouts, with_halo(): block = jnp.concatenate([low, block, high], axis=dim)  9.94 us
    ppermute x4, starting transfers between devices, with_halo(): lax.ppermute(lax.slice_in_dim(block, 0, width, axis=dim), axis, backward)  8.13 us
    ppermute x4, waiting for transfers between devices, with_halo(): lax.ppermute(lax.slice_in_dim(block, 0, width, axis=dim), axis, backward)  7.84 us
    ppermute x1, waiting for transfers between devices, shards(): lax.ppermute(surface_tile, 'gz', [(d, d ^ reach) for d in range(ways)])  6.98 us
    div x2, other arithmetic, rates(): (8.0 * (window(extended, 1, 0, 2) - window(extended, -1, 0, 2)) - (window...  4.83 us
    ppermute x4, starting transfers between devices, with_halo(): lax.ppermute(lax.slice_in_dim(block, block.shape[dim] - width, None, axis...  4.77 us
    concatenate x2, other arithmetic, with_halo(): block = jnp.concatenate([low, block, high], axis=dim)  3.41 us
  transfers between devices with their start and end apart: 10, of which 3 were waited for; matrix products, arithmetic and copies ran while one was open for 33% of the time, Pallas kernels for 0%

profile of v1, /device:TPU:1, one launch (start us, length us, event | category | flops | bytes accessed | tf_op | source)
XLA Modules:
  0.0 100.3 jit_solution(17135560402671369026)
XLA Ops:
  0.6 1.3 %fusion.87 = (f32[8,1,2048]{2,1,0:T(1,128)S(1)}, f32[8,1,2048]{2,1,0:T(1,128)S(1)}) fusion(f32[8,64,2048]{2,1,0:T(8,128)} %param.7), kind=kLoop, calls=%fused_computation.183 | loop fusion | bytes 262144 | tf_op jit(solution)/shard_map/slice | solution.py:17
  1.9 2.2 %collective-permute-start.6 = (f32[8,1,2048]{2,1,0:T(1,128)S(1)}, f32[8,1,2048]{2,1,0:T(1,128)S(1)}, u32[]{:S(2)}, u32[]{:S(2)}) collective-permute-start(f32[8,1,2048]{2,1,0:T(1,128)S(1)} %get-tuple-element.7), channel_id=1, source_target_pairs={{0,8},{8,16},{16,24},{24,0},{1,9},{9,17},{17,25},{25,1},{2,10},{10... | collective-permute-start | bytes 196616 | tf_op jit(solution)/shard_map/ppermute | solution.py:16
  4.1 2.1 %collective-permute-start.5 = (f32[8,1,2048]{2,1,0:T(1,128)S(1)}, f32[8,1,2048]{2,1,0:T(1,128)S(1)}, u32[]{:S(2)}, u32[]{:S(2)}) collective-permute-start(f32[8,1,2048]{2,1,0:T(1,128)S(1)} %get-tuple-element.8), channel_id=1, source_target_pairs={{8,0},{16,8},{24,16},{0,24},{9,1},{17,9},{25,17},{1,25},{10,2},{18... | collective-permute-start | bytes 196616 | tf_op jit(solution)/shard_map/ppermute | solution.py:19
  6.2 1.1 %pad_maximum_fusion.24 = f32[2,64,1024]{2,1,0:T(8,128)S(1)} fusion(f32[1,64,1024]{2,1,0:T(8,128)} %bitcast.74, f32[1,64,1024]{2,1,0:T(8,128)} %bitcast.76), kind=kLoop, calls=%fused_computation.173 | loop fusion | flops 131072 | bytes 1048576 | tf_op jit(solution)/shard_map/stack | solution.py:74
  7.3 1.3 %collective-permute-start = (f32[2,64,1024]{2,1,0:T(8,128)S(1)}, f32[2,64,1024]{2,1,0:T(8,128)S(1)}, u32[]{:S(2)}, u32[]{:S(2)}) collective-permute-start(f32[2,64,1024]{2,1,0:T(8,128)S(1)} %pad_maximum_fusion.24), channel_id=1, source_target_pairs={{0,1},{1,0},{2,3},{3,2},{4,5},{5,4},{6,7},{7,6},{8,9},{9,8},{10,11... | collective-permute-start | bytes 1572872 | tf_op jit(solution)/shard_map/ppermute | solution.py:80
  8.6 1.1 %multiply_bitcast_fusion = f32[1,64,2048]{2,1,0:T(8,128)S(1)} fusion(s32[64,2048]{1,0:T(8,128)} %param.6), kind=kLoop, calls=%fused_computation.175 | loop fusion | flops 262144 | bytes 1048576 | tf_op jit(solution)/shard_map/broadcast_in_dim | solution.py:85
  9.7 0.0 copy-start.7
  9.7 0.0 copy-start.8
  9.7 0.0 collective-permute-done.6
  9.7 0.0 collective-permute-done.5
  9.7 3.1 %pad_maximum_fusion = f32[8,66,2048]{2,1,0:T(8,128)S(1)} fusion(f32[8,1,2048]{2,1,0:T(1,128)S(1)} %collective-permute-done.5, f32[8,64,2048]{2,1,0:T(8,128)} %param.7, f32[8,1,2048]{2,1,0:T(1,128)S(1)} %collective-permute-done.6), kind=kLoop, calls=%fused_computation.16 | loop fusion | flops 2162688 | bytes 8650752 | tf_op jit(solution)/shard_map/concatenate | solution.py:20
  12.9 7.0 %collective-permute-done = f32[2,64,1024]{2,1,0:T(8,128)S(1)} collective-permute-done((f32[2,64,1024]{2,1,0:T(8,128)S(1)}, f32[2,64,1024]{2,1,0:T(8,128)S(1)}, u32[]{:S(2)}, u32[]{:S(2)}) %collective-permute-start) | collective-permute-done | bytes 524320 | tf_op jit(solution)/shard_map/ppermute | solution.py:80
  19.9 0.1 maximum_select_fusion
  20.0 0.7 pad_maximum_fusion.26
  20.7 3.3 %collective-permute-start.2 = (f32[3,5,2048]{2,1,0:T(8,128)S(1)}, f32[3,5,2048]{2,1,0:T(8,128)S(1)}, u32[]{:S(2)}, u32[]{:S(2)}) collective-permute-start(f32[3,5,2048]{2,1,0:T(8,128)S(1)} %get-tuple-element.16), channel_id=1, source_target_pairs={{8,0},{16,8},{24,16},{0,24},{9,1},{17,9},{25,17},{1,25},{10,2},{18... | collective-permute-start | bytes 368648 | tf_op jit(solution)/shard_map/ppermute | solution.py:19
  24.0 0.2 fusion.86
  24.1 2.4 %collective-permute-start.7 = (f32[8,66,1]{2,1,0:T(8,128)S(1)}, f32[8,66,1]{2,1,0:T(8,128)S(1)}, u32[]{:S(2)}, u32[]{:S(2)}) collective-permute-start(f32[8,66,1]{2,1,0:T(8,128)S(1)} %get-tuple-element.5), channel_id=1, source_target_pairs={{2,0},{4,2},{6,4},{0,6},{3,1},{5,3},{7,5},{1,7},{10,8},{12,10},{14... | collective-permute-start | bytes 6344 | tf_op jit(solution)/shard_map/ppermute | solution.py:19
  26.6 1.2 %collective-permute-start.8 = (f32[8,66,1]{2,1,0:T(8,128)S(1)}, f32[8,66,1]{2,1,0:T(8,128)S(1)}, u32[]{:S(2)}, u32[]{:S(2)}) collective-permute-start(f32[8,66,1]{2,1,0:T(8,128)S(1)} %get-tuple-element.6), channel_id=1, source_target_pairs={{0,2},{2,4},{4,6},{6,0},{1,3},{3,5},{5,7},{7,1},{8,10},{10,12},{12... | collective-permute-start | bytes 6344 | tf_op jit(solution)/shard_map/ppermute | solution.py:16
  27.7 0.5 add_multiply_fusion
  28.3 7.3 %collective-permute-done.7 = f32[8,66,1]{2,1,0:T(8,128)S(1)} collective-permute-done((f32[8,66,1]{2,1,0:T(8,128)S(1)}, f32[8,66,1]{2,1,0:T(8,128)S(1)}, u32[]{:S(2)}, u32[]{:S(2)}) %collective-permute-start.7) | collective-permute-done | bytes 2144 | tf_op jit(solution)/shard_map/ppermute | solution.py:19
  35.5 0.0 collective-permute-done.8
  35.5 7.0 %concatenate.64 = f32[8,66,2050]{2,1,0:T(8,128)} concatenate(f32[8,66,1]{2,1,0:T(8,128)S(1)} %collective-permute-done.8, f32[8,66,2048]{2,1,0:T(8,128)} %copy-done, f32[8,66,1]{2,1,0:T(8,128)S(1)} %collective-permute-done.7), dimensions={2} | concatenate | bytes 8659200 | tf_op jit(solution)/shard_map/concatenate | solution.py:20
  42.5 0.3 pad_maximum_fusion.11
  42.8 0.0 copy-start.2
  42.8 0.1 fusion.88
  42.9 0.4 collective-permute-start.4
  43.3 1.4 %collective-permute-start.3 = (f32[3,74,5]{2,1,0:T(8,128)S(1)}, f32[3,74,5]{2,1,0:T(8,128)}, u32[]{:S(2)}, u32[]{:S(2)}) collective-permute-start(f32[3,74,5]{2,1,0:T(8,128)S(1)} %get-tuple-element.14), channel_id=1, source_target_pairs={{0,2},{2,4},{4,6},{6,0},{1,3},{3,5},{5,7},{7,1},{8,10},{10,12},{12... | collective-permute-start | bytes 13328 | tf_op jit(solution)/shard_map/ppermute | solution.py:16
  44.7 2.2 %fusion.75 = f32[66,2050]{1,0:T(8,128)} fusion(f32[8,66,2050]{2,1,0:T(8,128)} %concatenate.64, pred[]{:T(512)S(6)} %eq.7), kind=kLoop, calls=%fused_computation.148 | loop fusion | flops 135300 | bytes 1623601 | tf_op jit(solution)/shard_map/jit(_where)/select_n | solution.py:101
  46.9 1.2 %collective-permute-start.9 = (f32[66,2050]{1,0:T(8,128)}, f32[66,2050]{1,0:T(8,128)}, u32[]{:S(2)}, u32[]{:S(2)}) collective-permute-start(f32[66,2050]{1,0:T(8,128)} %fusion.75), channel_id=1, source_target_pairs={{0,1},{1,0},{2,3},{3,2},{4,5},{5,4},{6,7},{7,6},{8,9},{9,8},{10,11... | collective-permute-start | bytes 1623608 | tf_op jit(solution)/shard_map/ppermute | solution.py:27
  48.1 0.6 collective-permute-done.4
  48.7 0.6 copy-done.9
  49.4 3.0 %concatenate.56 = f32[3,74,2058]{2,1,0:T(8,128)S(1)} concatenate(f32[3,74,5]{2,1,0:T(8,128)} %collective-permute-done.3, f32[3,74,2048]{2,1,0:T(8,128)} %copy-done.2, f32[3,74,5]{2,1,0:T(8,128)} %copy-done.9), dimensions={2} | concatenate | bytes 3655008 | tf_op jit(solution)/shard_map/concatenate | solution.py:20
  52.4 2.4 %fusion.41 = (f32[2,70,2054]{2,1,0:T(8,128)S(1)}, f32[2,70,2054]{2,1,0:T(8,128)S(1)}) fusion(f32[3,74,2058]{2,1,0:T(8,128)S(1)} %concatenate.56), kind=kLoop, calls=%fused_computation.78 | loop fusion | flops 2875600 | bytes 11502400 | tf_op jit(solution)/shard_map/div | solution.py:41
  54.8 0.3 fusion.61
  55.1 1.4 %fusion.65 = f32[1,70,2054]{2,1,0:T(8,128)S(1)} fusion(f32[2,70,2054]{2,1,0:T(8,128)S(1)} %get-tuple-element.10, f32[2,70,2054]{2,1,0:T(8,128)S(1)} %get-tuple-element.9, f32[74,2058]{1,0:T(8,128)S(1)} %slice_bitcast_fusion, f32[3,74,2058]{2,1,0:T(8,128)S(1)} %concatenate.56), kind=kLoop, calls=%fused_computation.127 | loop fusion | flops 3019380 | bytes 8051680 | tf_op jit(solution)/shard_map/stack | solution.py:70
  56.5 0.4 slice_add_fusion.1
  57.0 2.4 %fusion.33 = (f32[2,66,2050]{2,1,0:T(8,128)S(1)}, f32[2,66,2050]{2,1,0:T(8,128)S(1)}) fusion(f32[2,70,2054]{2,1,0:T(8,128)S(1)} %slice_add_fusion.1), kind=kLoop, calls=%fused_computation.65 | loop fusion | flops 2706000 | bytes 10824000 | tf_op jit(solution)/shard_map/div | solution.py:41
  59.4 0.3 fusion.47
  59.7 1.4 %fusion.51 = f32[1,66,2050]{2,1,0:T(8,128)S(1)} fusion(f32[2,66,2050]{2,1,0:T(8,128)S(1)} %get-tuple-element.18, f32[2,66,2050]{2,1,0:T(8,128)S(1)} %get-tuple-element.17, f32[70,2054]{1,0:T(8,128)S(1)} %slice_bitcast_fusion.3, f32[2,70,2054]{2,1,0:T(8,128)S(1)} %slice_add_fusion.1), kind=kLoop, calls=%fused_computation.100 | loop fusion | flops 2841300 | bytes 7576800 | tf_op jit(solution)/shard_map/stack | solution.py:70
  61.1 0.0 copy-start.10
  61.1 0.7 fusion.36
  61.9 0.2 slice_add_fusion.2
  62.1 0.3 slice.461
  62.5 2.5 %fusion.85 = (f32[64,2048]{1,0:T(8,128)}, f32[64,2048]{1,0:T(8,128)}) fusion(f32[3,5,2048]{2,1,0:T(8,128)S(1)} %collective-permute-done.1, f32[1,64,2048]{2,1,0:T(8,128)S(1)} %copy-done.4, f32[2,64,2048]{2,1,0:T(8,128)S(1)} %maximum_select_fusion, f32[3,5,2048]{2,1,0:T(8,128)S(1)} %collective-permute-done.2, f32[3,74,5]{2,1,0:T(8,128)} %collective-permute-done.3, ...), kind=kLoop, calls=%fused_computation.169 | loop fusion | flops 2097152 | bytes 2876080 | tf_op jit(solution)/shard_map/sub | solution.py:116
  65.0 0.8 dynamic-slice_bitcast_fusion
  65.8 2.0 %fusion.82 = (f32[64,2048]{1,0:T(8,128)}, f32[64,2048]{1,0:T(8,128)}, f32[64,2048]{1,0:T(8,128)}, f32[64,2048]{1,0:T(8,128)}) fusion(f32[1,66,2050]{2,1,0:T(8,128)S(1)} %slice_add_fusion.2), kind=kLoop, calls=%fused_computation.165 | loop fusion | flops 786432 | bytes 4718592 | tf_op jit(solution)/shard_map/mul | solution.py:116
  67.8 2.1 %fusion.46 = (f32[1,66,2050]{2,1,0:T(8,128)S(1)}, f32[1,66,2050]{2,1,0:T(8,128)}) fusion(f32[66,2050]{1,0:T(8,128)} %collective-permute-done.9, f32[2,66,2050]{2,1,0:T(8,128)S(1)} %fusion.36, f32[8,66,2050]{2,1,0:T(8,128)S(1)} %bitcast.73, pred[]{:T(512)S(6)} %eq.7), kind=kLoop, calls=%fused_computation.90 | loop fusion | flops 541200 | bytes 3247201 | tf_op jit(solution)/shard_map/broadcast_in_dim | solution.py:105
  69.9 30.2 %fusion.5 = f32[8,64,2048]{2,1,0:T(8,128)} fusion(f32[8,66,2050]{2,1,0:T(8,128)S(1)} %bitcast.73, f32[1,66,2050]{2,1,0:T(8,128)} %get-tuple-element.4, f32[1,66,2050]{2,1,0:T(8,128)S(1)} %get-tuple-element.3, f32[8,66,1]{2,1,0:T(8,128)} %copy-done.6, f32[8,1,2048]{2,1,0:T(1,128)} %copy-done.13, f32[8,64,2048]{2,1,0:T(8,128)S(1)} %copy-done.1, ...), kind=kLoop, calls=%fused_computation.22 | loop fusion | flops 55574528 | bytes 17081664 | tf_op jit(solution)/shard_map/add | solution.py:144
  (35 shorter events, 0.2 us)
Async XLA Ops:
  1.9 7.8 %collective-permute-start.6 = (f32[8,1,2048]{2,1,0:T(1,128)S(1)}, f32[8,1,2048]{2,1,0:T(1,128)S(1)}, u32[]{:S(2)}, u32[]{:S(2)}) collective-permute-start(f32[8,1,2048]{2,1,0:T(1,128)S(1)} %get-tuple-element.7), channel_id=1, source_target_pairs={{0,8},{8,16},{16,24},{24,0},{1,9},{9,17},{17,25},{25,1},{2,10},{10... | collective-permute-start | bytes 196616 | tf_op jit(solution)/shard_map/ppermute | solution.py:16
  4.1 5.6 %collective-permute-start.5 = (f32[8,1,2048]{2,1,0:T(1,128)S(1)}, f32[8,1,2048]{2,1,0:T(1,128)S(1)}, u32[]{:S(2)}, u32[]{:S(2)}) collective-permute-start(f32[8,1,2048]{2,1,0:T(1,128)S(1)} %get-tuple-element.8), channel_id=1, source_target_pairs={{8,0},{16,8},{24,16},{0,24},{9,1},{17,9},{25,17},{1,25},{10,2},{18... | collective-permute-start | bytes 196616 | tf_op jit(solution)/shard_map/ppermute | solution.py:19
  7.3 12.6 %collective-permute-start = (f32[2,64,1024]{2,1,0:T(8,128)S(1)}, f32[2,64,1024]{2,1,0:T(8,128)S(1)}, u32[]{:S(2)}, u32[]{:S(2)}) collective-permute-start(f32[2,64,1024]{2,1,0:T(8,128)S(1)} %pad_maximum_fusion.24), channel_id=1, source_target_pairs={{0,1},{1,0},{2,3},{3,2},{4,5},{5,4},{6,7},{7,6},{8,9},{9,8},{10,11... | collective-permute-start | bytes 1572872 | tf_op jit(solution)/shard_map/ppermute | solution.py:80
  9.6 32.8 %copy-start.3 = (f32[1,64,2048]{2,1,0:T(8,128)}, f32[1,64,2048]{2,1,0:T(8,128)S(1)}, u32[]{:S(2)}) copy-start(f32[1,64,2048]{2,1,0:T(8,128)S(1)} %multiply_bitcast_fusion) | copy-start | bytes 1572868
  9.7 10.2 %copy-start.7 = (f32[64,1024]{1,0:T(8,128)S(1)}, f32[64,1024]{1,0:T(8,128)}, u32[]{:S(2)}) copy-start(f32[64,1024]{1,0:T(8,128)} %param.5) | copy-start | bytes 786436
  9.7 10.2 %copy-start.8 = (f32[64,1024]{1,0:T(8,128)S(1)}, f32[64,1024]{1,0:T(8,128)}, u32[]{:S(2)}) copy-start(f32[64,1024]{1,0:T(8,128)} %param.4) | copy-start | bytes 786436
  9.7 3.1 %copy-start.11 = (f32[8,1,2048]{2,1,0:T(1,128)}, f32[8,1,2048]{2,1,0:T(1,128)S(1)}, u32[]{:S(2)}) copy-start(f32[8,1,2048]{2,1,0:T(1,128)S(1)} %collective-permute-done.6) | copy-start | bytes 196612
  9.7 3.1 %copy-start.13 = (f32[8,1,2048]{2,1,0:T(1,128)}, f32[8,1,2048]{2,1,0:T(1,128)S(1)}, u32[]{:S(2)}) copy-start(f32[8,1,2048]{2,1,0:T(1,128)S(1)} %collective-permute-done.5) | copy-start | bytes 196612
  12.9 11.1 %copy-start = (f32[8,66,2048]{2,1,0:T(8,128)}, f32[8,66,2048]{2,1,0:T(8,128)S(1)}, u32[]{:S(2)}) copy-start(f32[8,66,2048]{2,1,0:T(8,128)S(1)} %pad_maximum_fusion) | copy-start | bytes 12976132
  20.7 21.8 %collective-permute-start.1 = (f32[3,5,2048]{2,1,0:T(8,128)}, f32[3,5,2048]{2,1,0:T(8,128)S(1)}, u32[]{:S(2)}, u32[]{:S(2)}) collective-permute-start(f32[3,5,2048]{2,1,0:T(8,128)} %get-tuple-element.15), channel_id=1, source_target_pairs={{0,8},{8,16},{16,24},{24,0},{1,9},{9,17},{17,25},{25,1},{2,10},{10... | collective-permute-start | bytes 368648 | tf_op jit(solution)/shard_map/ppermute | solution.py:16
  20.7 21.8 %collective-permute-start.2 = (f32[3,5,2048]{2,1,0:T(8,128)S(1)}, f32[3,5,2048]{2,1,0:T(8,128)S(1)}, u32[]{:S(2)}, u32[]{:S(2)}) collective-permute-start(f32[3,5,2048]{2,1,0:T(8,128)S(1)} %get-tuple-element.16), channel_id=1, source_target_pairs={{8,0},{16,8},{24,16},{0,24},{9,1},{17,9},{25,17},{1,25},{10,2},{18... | collective-permute-start | bytes 368648 | tf_op jit(solution)/shard_map/ppermute | solution.py:19
  24.1 11.4 %collective-permute-start.7 = (f32[8,66,1]{2,1,0:T(8,128)S(1)}, f32[8,66,1]{2,1,0:T(8,128)S(1)}, u32[]{:S(2)}, u32[]{:S(2)}) collective-permute-start(f32[8,66,1]{2,1,0:T(8,128)S(1)} %get-tuple-element.5), channel_id=1, source_target_pairs={{2,0},{4,2},{6,4},{0,6},{3,1},{5,3},{7,5},{1,7},{10,8},{12,10},{14... | collective-permute-start | bytes 6344 | tf_op jit(solution)/shard_map/ppermute | solution.py:19
  26.6 8.9 %collective-permute-start.8 = (f32[8,66,1]{2,1,0:T(8,128)S(1)}, f32[8,66,1]{2,1,0:T(8,128)S(1)}, u32[]{:S(2)}, u32[]{:S(2)}) collective-permute-start(f32[8,66,1]{2,1,0:T(8,128)S(1)} %get-tuple-element.6), channel_id=1, source_target_pairs={{0,2},{2,4},{4,6},{6,0},{1,3},{3,5},{5,7},{7,1},{8,10},{10,12},{12... | collective-permute-start | bytes 6344 | tf_op jit(solution)/shard_map/ppermute | solution.py:16
  35.5 7.0 %copy-start.5 = (f32[8,66,1]{2,1,0:T(8,128)}, f32[8,66,1]{2,1,0:T(8,128)S(1)}, u32[]{:S(2)}) copy-start(f32[8,66,1]{2,1,0:T(8,128)S(1)} %collective-permute-done.7) | copy-start | bytes 6340
  35.5 7.0 %copy-start.6 = (f32[8,66,1]{2,1,0:T(8,128)}, f32[8,66,1]{2,1,0:T(8,128)S(1)}, u32[]{:S(2)}) copy-start(f32[8,66,1]{2,1,0:T(8,128)S(1)} %collective-permute-done.8) | copy-start | bytes 6340
  42.8 5.9 %copy-start.2 = (f32[3,74,2048]{2,1,0:T(8,128)}, f32[3,74,2048]{2,1,0:T(8,128)S(1)}, u32[]{:S(2)}) copy-start(f32[3,74,2048]{2,1,0:T(8,128)S(1)} %pad_maximum_fusion.11) | copy-start | bytes 5455876
  42.9 5.8 %collective-permute-start.4 = (f32[3,74,5]{2,1,0:T(8,128)S(1)}, f32[3,74,5]{2,1,0:T(8,128)S(1)}, u32[]{:S(2)}, u32[]{:S(2)}) collective-permute-start(f32[3,74,5]{2,1,0:T(8,128)S(1)} %get-tuple-element.13), channel_id=1, source_target_pairs={{2,0},{4,2},{6,4},{0,6},{3,1},{5,3},{7,5},{1,7},{10,8},{12,10},{14... | collective-permute-start | bytes 13328 | tf_op jit(solution)/shard_map/ppermute | solution.py:19
  43.3 6.1 %collective-permute-start.3 = (f32[3,74,5]{2,1,0:T(8,128)S(1)}, f32[3,74,5]{2,1,0:T(8,128)}, u32[]{:S(2)}, u32[]{:S(2)}) collective-permute-start(f32[3,74,5]{2,1,0:T(8,128)S(1)} %get-tuple-element.14), channel_id=1, source_target_pairs={{0,2},{2,4},{4,6},{6,0},{1,3},{3,5},{5,7},{7,1},{8,10},{10,12},{12... | collective-permute-start | bytes 13328 | tf_op jit(solution)/shard_map/ppermute | solution.py:16
  46.9 20.9 %collective-permute-start.9 = (f32[66,2050]{1,0:T(8,128)}, f32[66,2050]{1,0:T(8,128)}, u32[]{:S(2)}, u32[]{:S(2)}) collective-permute-start(f32[66,2050]{1,0:T(8,128)} %fusion.75), channel_id=1, source_target_pairs={{0,1},{1,0},{2,3},{3,2},{4,5},{5,4},{6,7},{7,6},{8,9},{9,8},{10,11... | collective-permute-start | bytes 1623608 | tf_op jit(solution)/shard_map/ppermute | solution.py:27
  48.7 0.6 copy-start.9
  61.1 1.4 %copy-start.4 = (f32[1,64,2048]{2,1,0:T(8,128)S(1)}, f32[1,64,2048]{2,1,0:T(8,128)}, u32[]{:S(2)}) copy-start(f32[1,64,2048]{2,1,0:T(8,128)} %copy-done.3) | copy-start | bytes 1572868
  61.1 1.4 %copy-start.10 = (f32[3,74,5]{2,1,0:T(8,128)S(1)}, f32[3,74,5]{2,1,0:T(8,128)}, u32[]{:S(2)}) copy-start(f32[3,74,5]{2,1,0:T(8,128)} %copy-done.9) | copy-start | bytes 13324
  61.9 5.9 %slice-start = ((s8[5013504]{0:T(1024)(128)(4,1)}), s8[4194304]{0:T(1024)(128)(4,1)S(1)}, s32[]{:S(2)}) async-start(s8[5013504]{0:T(1024)(128)(4,1)} %bitcast.72), calls=%async_computation | async-start | bytes 8388608
  62.5 5.3 %slice-start.1 = ((s8[5013504]{0:T(1024)(128)(4,1)}), s8[819200]{0:T(1024)(128)(4,1)S(1)}, s32[]{:S(2)}) async-start(s8[5013504]{0:T(1024)(128)(4,1)} %bitcast.72), calls=%async_computation.1 | async-start | bytes 1638400
  65.8 4.1 %copy-start.1 = (f32[8,64,2048]{2,1,0:T(8,128)S(1)}, f32[8,64,2048]{2,1,0:T(8,128)}, u32[]{:S(2)}) copy-start(f32[8,64,2048]{2,1,0:T(8,128)} %param.7) | copy-start | bytes 12582916
  65.8 4.1 %copy-start.12 = (f32[8,1,2048]{2,1,0:T(1,128)S(1)}, f32[8,1,2048]{2,1,0:T(1,128)}, u32[]{:S(2)}) copy-start(f32[8,1,2048]{2,1,0:T(1,128)} %copy-done.11) | copy-start | bytes 196612
